TPU v7x, 256 devices: a whole 4x4x8 slice. The times are simulated.
256 devices in a mesh: frame: 16 (over y, x), seq: 16 (over z, core).
Axes of the slice: x: 4, y: 4, z: 8, core: 2. Of those that a mesh axis runs over, the one named last changes fastest.
Arguments:
- tokens: bfloat16 [16, 512, 5120], P('frame', 'seq'), may hold values from -6 to 6
- query_rows: bfloat16 [16, 512, 4096], P('frame', 'seq'), may hold values from -40 to 40
- key_rows: bfloat16 [16, 512, 4096], P('frame', 'seq'), may hold values from -40 to 40
- value_rows: bfloat16 [16, 512, 4096], P('frame', 'seq'), may hold values from -6 to 6
- gain_query: float32 [4096], replicated, may hold values from 0.5 to 2.5
- gain_key: float32 [4096], replicated, may hold values from 0.5 to 2.5
- out_weight: bfloat16 [4096, 5120], P('seq'), may hold values from -0.09375 to 0.09375
- out_bias: bfloat16 [5120], replicated, may hold values from -3 to 3
- gate_table: bfloat16 [64, 5120], replicated, may hold values from -12 to 12
- noise_level: int32 [16], replicated, may hold values from 0 to 63
- slot_order: int32 [16], replicated, may hold values from 0 to 1023, as said below
Outputs:
- updated: bfloat16 [16, 512, 5120], P('frame', 'seq')
Inputs may be any that keep to these rules, and one draw needn't show every extreme that they name: `slot_order`: all 16 stamps are distinct.
All inputs are finite; a program needn't handle non-finite values.
Results may differ from a plain program's by a relative error of at most 0.013.
Values may be sent and summed in bfloat16 or wider, within the bound.
A program may use at most 64 MiB of HBM per device.

v0:
```python
import functools

import jax
import jax.numpy as jnp
from jax import lax
from jax.experimental import pallas as pl
from jax.experimental.pallas import tpu as pltpu
from jax.sharding import PartitionSpec as P

HD = 128
EPS = 1e-06
X, Y, Z = 4, 4, 8
ROWS = 32
HALVES = 2
HROWS = ROWS // HALVES
QROWS = X * Z * HROWS
FROWS = Z * HROWS
GROUP = X * Z * ROWS
KROWS = Z * ROWS
D = 5120
DEPTH = 512
SUBS = 4
SUB = D // SUBS
STEPS = Z // 2
MESH = pl.DeviceIdType.MESH
SCALE = HD ** -0.5 * 1.4426950408889634
HIDDEN = -1e30


def position():
    frame = lax.axis_index("frame")
    seq = lax.axis_index("seq")
    return lax.rem(frame, X), frame // X, seq // 2, lax.rem(seq, 2)


def device(x, y, z, c):
    return (y * X + x, z * 2 + c)


def remote(src, dst, send, recv, dev):
    return pltpu.make_async_remote_copy(
        src_ref=src, dst_ref=dst, send_sem=send, recv_sem=recv, device_id=dev, device_id_type=MESH
    )


def plane_peer(d, x, z):
    return lax.rem(x + lax.rem(d, X), X), lax.rem(z + d // X, Z)


def normalize_into(rows_ref, gain_ref, out_ref):
    values = rows_ref[...].astype(jnp.float32)
    inverse = lax.rsqrt(jnp.mean(values * values, axis=-1, keepdims=True) + EPS)
    for h in range(X * Z):
        at = slice(h * HD, (h + 1) * HD)
        part = (rows_ref[:, at].astype(jnp.float32) * inverse * gain_ref[:, at]).astype(jnp.bfloat16)
        out_ref[h] = part.reshape(out_ref.shape[1:])


def fused_kernel(
    stamp_ref, level_ref, q_ref, k_ref, v_ref, gq_ref, gk_ref, w_hbm, tok_hbm, bias_hbm, gate_hbm,
    out_ref,
    qn, kn, qb, kb, vb, top_ref, sum_ref, acc_ref, att, a_ref, w_ref, part, held, tok_ref, bias_ref, gate_ref,
    a2a_send, a2a_recv, own_sem, near_send, near_recv, far_send, far_recv, swap_send, swap_recv,
    w_sem, load_sem, x_send, x_recv, ring_send, ring_recv,
):
    x, y, z, c = position()
    up, down, opposite = lax.rem(y + 1, Y), lax.rem(y + Y - 1, Y), lax.rem(y + 2, Y)
    partner = device(x, y, z, 1 - c)
    dev_up, dev_down = device(x, up, z, c), device(x, down, z, c)
    next_z, last_z = device(x, y, lax.rem(z + 1, Z), c), device(x, y, lax.rem(z + Z - 1, Z), c)
    groups = (y, down, up, opposite)
    bufs = (kb, vb)

    barrier = pltpu.get_barrier_semaphore()

    def greet(i, carry):
        tx, tz = plane_peer(i + 1, x, z)
        pl.semaphore_signal(barrier, inc=1, device_id=device(tx, y, tz, c), device_id_type=MESH)
        return carry

    lax.fori_loop(0, X * Z - 1, greet, 0)
    for dev in (dev_up, dev_down, partner):
        pl.semaphore_signal(barrier, inc=1, device_id=dev, device_id_type=MESH)
    w_rows = w_ref.at[pl.ds(pl.multiple_of(c * (DEPTH // 2), DEPTH // 2), DEPTH // 2)]
    loads = [
        pltpu.make_async_copy(source, target, load_sem.at[i])
        for i, (source, target) in enumerate(
            ((w_hbm, w_rows), (tok_hbm, tok_ref), (bias_hbm, bias_ref), (gate_hbm, gate_ref))
        )
    ]
    for load in loads:
        load.start()
    normalize_into(k_ref, gk_ref, kn)
    pl.semaphore_wait(barrier, X * Z - 1 + 3)

    slot = pl.ds(pl.multiple_of((x * Z + z) * ROWS, ROWS), ROWS)

    def scatter(kind, source, target):
        def send(i, carry):
            tx, tz = plane_peer(i + 1, x, z)
            remote(
                source(tz * X + tx), target, a2a_send.at[kind], a2a_recv.at[kind], device(tx, y, tz, c)
            ).start()
            return carry

        lax.fori_loop(0, X * Z - 1, send, 0)
        own = pltpu.make_async_copy(source(z * X + x), target, own_sem.at[kind])
        own.start()
        return own

    def all_of(kind, sem):
        rest = kb.at[0, 0, pl.ds(0, GROUP - ROWS)]
        pltpu.make_async_copy(rest, rest, sem.at[kind]).wait()

    own = [
        scatter(0, lambda h: kn.at[h], kb.at[c, y, slot]),
        scatter(1, lambda h: v_ref.at[:, pl.ds(pl.multiple_of(h * HD, HD), HD)], vb.at[c, y, slot]),
    ]
    normalize_into(q_ref, gq_ref, qn)
    own.append(scatter(2, lambda h: qn.at[h], qb.at[x, :, z]))
    w_swap = remote(w_hbm, w_rows, w_sem.at[0], w_sem.at[1], partner)
    w_swap.start()

    half = GROUP // 2

    def near(t, i):
        block = bufs[t].at[c, y]
        return remote(block, block, near_send.at[t, i], near_recv.at[t, i], (dev_up, dev_down)[i])

    def far(t, i):
        block = bufs[t].at[c, (down, up)[i], pl.ds(i * half, half)]
        return remote(block, block, far_send.at[t, i], far_recv.at[t, i], (dev_up, dev_down)[i])

    def swap(t, i):
        block = bufs[t].at[c, groups[i]]
        return remote(block, block, swap_send.at[t, i], swap_recv.at[t, i], partner)

    def pass_own(t):
        own[t].wait()
        all_of(t, a2a_recv)
        near(t, 0).start()
        near(t, 1).start()
        swap(t, 0).start()

    def pass_near(t):
        near(t, 0).wait_recv()
        far(t, 0).start()
        swap(t, 1).start()
        near(t, 1).wait_recv()
        far(t, 1).start()
        swap(t, 2).start()

    def pass_far(t):
        far(t, 0).wait_recv()
        far(t, 1).wait_recv()
        swap(t, 3).start()

    def attend(hh, yy):
        query = qb[:, hh].reshape(QROWS, HD)
        scores = [
            lax.dot_general(
                query, kb[core, yy], (((1,), (1,)), ((), ())), preferred_element_type=jnp.float32
            )
            for core in range(2)
        ]
        key_stamp = [stamp_ref[yy * X + f] for f in range(X)]
        summed = [None, None]
        weights = [[], []]
        alphas = []
        for g in range(X):
            stamp = stamp_ref[y * X + g]
            rows = slice(g * FROWS, (g + 1) * FROWS)
            best = jnp.full((FROWS, 128), 2 * HIDDEN, jnp.float32)
            shift = [jnp.where(key_stamp[f] <= stamp, 0.0, HIDDEN) for f in range(X)]
            for f in range(X):
                seen = None
                for core in range(2):
                    for i in range(f * KROWS, (f + 1) * KROWS, 128):
                        tile = scores[core][rows, i : i + 128]
                        seen = tile if seen is None else jnp.maximum(seen, tile)
                best = jnp.maximum(best, seen + shift[f])
            old = top_ref[hh, rows, :]
            new = jnp.maximum(old, jnp.max(best, axis=-1, keepdims=True) * SCALE)
            alpha = jnp.exp2(old - new)
            top_ref[hh, rows, :] = new
            total = sum_ref[hh, rows, :] * alpha
            column = new[:, 0:1]
            for core in range(2):
                row_weights = []
                for f in range(X):
                    piece = scores[core][rows, f * KROWS : (f + 1) * KROWS]
                    exponent = jnp.exp2(piece * SCALE + (shift[f] - column))
                    for i in range(0, KROWS, 128):
                        total = total + exponent[:, i : i + 128]
                    row_weights.append(exponent.astype(jnp.bfloat16))
                weights[core].append(jnp.concatenate(row_weights, axis=1))
            sum_ref[hh, rows, :] = total
            alphas.append(alpha)
        gained = sum(
            jnp.dot(
                jnp.concatenate(weights[core], axis=0), vb[core, yy], preferred_element_type=jnp.float32
            )
            for core in range(2)
        )
        acc_ref[hh] = acc_ref[hh] * jnp.concatenate(alphas, axis=0) + gained

    def cross(hh, d):
        tx = lax.rem(x + d, X)
        columns = pl.ds(pl.multiple_of(x * HD, HD), HD)
        return remote(
            att.at[hh, tx], a_ref.at[hh, :, columns], x_send.at[hh, d], x_recv.at[hh, d], device(tx, y, z, c)
        )

    def cross_own(hh):
        columns = pl.ds(pl.multiple_of(x * HD, HD), HD)
        return pltpu.make_async_copy(att.at[hh, x], a_ref.at[hh, :, columns], x_send.at[hh, 0])

    def finish(hh):
        total = jnp.sum(sum_ref[hh], axis=-1, keepdims=True)
        att[hh] = (acc_ref[hh] / total).astype(jnp.bfloat16).reshape(X, FROWS, HD)
        for d in range(1, X):
            cross(hh, d).start()
        cross_own(hh).start()

    def chunk(way, step):
        index = lax.rem(z + STEPS - step, Z) if way == 0 else lax.rem(z + STEPS + step, Z)
        return pl.ds(pl.multiple_of(index * HROWS, HROWS), HROWS)

    def opens(way, sub):
        return 0 if sub // (SUBS // 2) == way else 1

    def ring(hh, way, sub, step):
        where = pl.ds(sub * SUB, SUB)
        if step == opens(way, sub):
            source = part.at[hh, chunk(way, step), where]
        else:
            source = held.at[hh, way, step - 1, :, where]
        at = (hh, way, sub, step)
        return remote(
            source, held.at[hh, way, step, :, where], ring_send.at[at], ring_recv.at[at], (next_z, last_z)[way]
        )

    pairs = [(way, sub) for sub in range(SUBS // 2) for way, sub in ((0, sub), (1, sub + SUBS // 2))]
    pairs += [(1 - way, sub) for way, sub in pairs]

    def project(hh):
        for d in range(1, X):
            cross(hh, d).wait_recv()
        cross_own(hh).wait()
        for sub in range(SUBS):
            where = pl.ds(sub * SUB, SUB)
            part[hh, :, where] = jnp.dot(
                a_ref[hh], w_ref[:, where], preferred_element_type=jnp.float32
            ).astype(jnp.bfloat16)
            ring(hh, sub // (SUBS // 2), sub, 0).start()
        for sub in range(SUBS):
            ring(hh, 1 - sub // (SUBS // 2), sub, 1).start()

    def relay(hh, step):
        for way, sub in pairs:
            if step > opens(way, sub):
                ring(hh, way, sub, step - 1).wait_recv()
                where = pl.ds(sub * SUB, SUB)
                mine = part[hh, chunk(way, step), where].astype(jnp.float32)
                came = held[hh, way, step - 1, :, where].astype(jnp.float32)
                held[hh, way, step - 1, :, where] = (came + mine).astype(jnp.bfloat16)
                ring(hh, way, sub, step).start()

    def settle(hh):
        rows = pl.ds(hh * HROWS, HROWS)
        mine_rows = pl.ds(pl.multiple_of(z * HROWS, HROWS), HROWS)
        for sub in range(SUBS):
            where = pl.ds(sub * SUB, SUB)
            projected = part[hh, mine_rows, where].astype(jnp.float32)
            for way in range(2):
                ring(hh, way, sub, STEPS - 1).wait_recv()
                projected = projected + held[hh, way, STEPS - 1, :, where].astype(jnp.float32)
            gate = jnp.dot(hot, gate_ref[:, where], preferred_element_type=jnp.float32)[0:1]
            mixed = tok_ref[rows, where].astype(jnp.float32) + gate * (
                projected + bias_ref[:, where].astype(jnp.float32)
            )
            out_ref[rows, where] = mixed.astype(jnp.bfloat16)

    top_ref[...] = jnp.full_like(top_ref, 2 * HIDDEN)
    sum_ref[...] = jnp.zeros_like(sum_ref)
    acc_ref[...] = jnp.zeros_like(acc_ref)
    pass_own(0)
    pass_own(1)
    pass_near(0)
    own[2].wait()
    all_of(2, a2a_recv)
    pass_far(0)

    def wait_swap(i):
        swap(0, i).wait_recv()
        swap(1, i).wait_recv()

    order = ((0, 0), (0, 1), (0, 2), (1, 0), (0, 3), (1, 1), (1, 2), (1, 3))

    def choose(i, options):
        value = options[0]
        for n in range(1, len(options)):
            value = jnp.where(i == n, options[n], value)
        return value

    def step(i, carry):
        @pl.when(i == 0)
        def _():
            wait_swap(0)

        @pl.when(i == 1)
        def _():
            pass_near(1)
            wait_swap(1)

        @pl.when(i == 2)
        def _():
            wait_swap(2)

        @pl.when(i == 4)
        def _():
            pass_far(1)
            wait_swap(3)

        attend(choose(i, [hh for hh, _ in order]), choose(i, [groups[p] for _, p in order]))

        @pl.when(i == 4)
        def _():
            finish(0)

        @pl.when(i == 5)
        def _():
            for load in loads:
                load.wait()
            w_swap.wait()
            project(0)

        @pl.when(i == 6)
        def _():
            relay(0, 1)

        return carry

    lax.fori_loop(0, len(order), step, 0)
    finish(1)
    relay(0, 2)
    project(1)
    level = level_ref[lax.axis_index("frame")]
    hot = (lax.broadcasted_iota(jnp.int32, (8, gate_ref.shape[0]), 1) == level).astype(jnp.bfloat16)
    relay(0, 3)
    relay(1, 1)
    settle(0)
    relay(1, 2)
    relay(1, 3)
    settle(1)

    for t in range(2):
        for i in range(2):
            near(t, i).wait_send()
            far(t, i).wait_send()
        for i in range(4):
            swap(t, i).wait_send()
    for kind in range(3):
        all_of(kind, a2a_send)
    for hh in range(HALVES):
        for d in range(1, X):
            cross(hh, d).wait_send()
        for way in range(2):
            for sub in range(SUBS):
                for s in range(opens(way, sub), STEPS):
                    ring(hh, way, sub, s).wait_send()


def shards(
    tokens, query_rows, key_rows, value_rows, gain_query, gain_key,
    out_weight, out_bias, gate_table, noise_level, slot_order,
):
    vmem = pl.BlockSpec(memory_space=pltpu.VMEM)
    hbm = pl.BlockSpec(memory_space=pl.ANY)
    smem = pl.BlockSpec(memory_space=pltpu.SMEM)
    bf16, f32 = jnp.bfloat16, jnp.float32
    dma = pltpu.SemaphoreType.DMA
    out = pl.pallas_call(
        fused_kernel,
        out_shape=jax.ShapeDtypeStruct((ROWS, D), bf16),
        in_specs=[smem, smem] + [vmem] * 5 + [hbm] * 4,
        out_specs=vmem,
        scratch_shapes=[
            pltpu.VMEM((X * Z, HALVES, HROWS, HD), bf16),
            pltpu.VMEM((X * Z, ROWS, HD), bf16),
            pltpu.VMEM((X, HALVES, Z, HROWS, HD), bf16),
            pltpu.VMEM((2, Y, GROUP, HD), bf16),
            pltpu.VMEM((2, Y, GROUP, HD), bf16),
            pltpu.VMEM((HALVES, QROWS, 128), f32),
            pltpu.VMEM((HALVES, QROWS, 128), f32),
            pltpu.VMEM((HALVES, QROWS, HD), f32),
            pltpu.VMEM((HALVES, X, FROWS, HD), bf16),
            pltpu.VMEM((HALVES, FROWS, DEPTH), bf16),
            pltpu.VMEM((DEPTH, D), bf16),
            pltpu.VMEM((HALVES, FROWS, D), bf16),
            pltpu.VMEM((HALVES, 2, STEPS, HROWS, D), bf16),
            pltpu.VMEM((ROWS, D), bf16),
            pltpu.VMEM((1, D), bf16),
            pltpu.VMEM(gate_table.shape, bf16),
            dma((3,)), dma((3,)), dma((3,)),
            dma((2, 2)), dma((2, 2)), dma((2, 2)), dma((2, 2)), dma((2, 4)), dma((2, 4)),
            dma((2,)), dma((4,)), dma((HALVES, X)), dma((HALVES, X)),
            dma((HALVES, 2, SUBS, STEPS)), dma((HALVES, 2, SUBS, STEPS)),
        ],
        compiler_params=pltpu.CompilerParams(
            collective_id=0, has_side_effects=True, vmem_limit_bytes=56 * 2**20
        ),
        name="fused",
    )(
        slot_order.astype(jnp.int32), noise_level.astype(jnp.int32),
        query_rows[0], key_rows[0], value_rows[0], gain_query[None], gain_key[None],
        out_weight, tokens[0], out_bias[None], gate_table,
    )
    return out[None]


def solution(mesh):
    placed = (
        P("frame", "seq", None), P("frame", "seq", None), P("frame", "seq", None), P("frame", "seq", None),
        P(), P(), P("seq", None), P(), P(), P(), P(),
    )
    return jax.shard_map(
        shards, mesh=mesh, in_specs=placed, out_specs=P("frame", "seq", None), check_vma=False
    )
```

profile of v0, /device:TPU:24, one launch (start us, length us, event | category | flops | bytes accessed | tf_op | source)
XLA Modules:
  0.0 89.1 jit_solution(11150645031966960898)
XLA Ops:
  0.0 1.3 %broadcast_in_dim.14.bias_hbm = bf16[1,5120]{1,0:T(2,128)(2,1)} reshape(bf16[5120]{0:T(1024)(128)(2,1)} %param.18) | data formatting | bytes 20480 | tf_op jit(solution)/shard_map/broadcast_in_dim | solution.py:417
  1.3 86.0 %fused.1 = bf16[32,5120]{1,0:T(8,128)(2,1)} custom-call(s32[16]{0:T(128)} %stamp_ref.1, s32[16]{0:T(128)} %level_ref.1, bf16[32,4096]{1,0:T(8,128)(2,1)} %bitcast.9, bf16[32,4096]{1,0:T(8,128)(2,1)} %bitcast.10, bf16[32,4096]{1,0:T(8,128)(2,1)} %bitcast.11, f32[1,4096]{1,0:T(1,128)} %bitcast.12, f32[1,4096]{1,0:T(1,128)} %bitcast.13, ...), custom_call_target="tpu_custom_call" | custom-call | tf_op jit(solution)/shard_map/fused/pallas_call | solution.py:383
  87.4 1.7 %copy.13 = bf16[1,32,5120]{2,1,0:T(8,128)(2,1)} copy(bf16[1,32,5120]{2,1,0:T(8,128)(2,1)} %bitcast.7) | data formatting | bytes 655360
where the time goes:
time: 90 us; the launch traced here: 89.1 us
  Pallas kernels  86 us (96%)
  local copies, waits for them, and re-layouts  3.04 us (3%)
    pallas_call x1, Pallas kernels, shards(): pl.pallas_call(fused_kernel, out_shape=jax.ShapeDtypeStruct((ROWS, D), bf...  86 us

commit v1 on v0

--- a/solution.py
+++ b/solution.py
@@ -16,7 +16,9 @@
 QROWS = X * Z * HROWS
 FROWS = Z * HROWS
 GROUP = X * Z * ROWS
-KROWS = Z * ROWS
+PARTS = 2
+PART = GROUP // PARTS
+WIDE = X // PARTS
 D = 5120
 DEPTH = 512
 SUBS = 4
@@ -57,9 +59,9 @@
 
 
 def fused_kernel(
-    stamp_ref, level_ref, q_ref, k_ref, v_ref, gq_ref, gk_ref, w_hbm, tok_hbm, bias_hbm, gate_hbm,
+    stamp_hbm, level_hbm, q_hbm, k_hbm, v_hbm, gq_hbm, gk_hbm, w_hbm, tok_hbm, bias_hbm, gate_hbm,
     out_ref,
-    qn, kn, qb, kb, vb, top_ref, sum_ref, acc_ref, att, a_ref, w_ref, part, held, tok_ref, bias_ref, gate_ref,
+    stamp_ref, level_ref, q_ref, k_ref, gq_ref, gk_ref, qn, kn, qb, kb, vb, top_ref, sum_ref, acc_ref, att, a_ref, w_ref, part, held, tok_ref, bias_ref, gate_ref, bias_row, gate_row,
     a2a_send, a2a_recv, own_sem, near_send, near_recv, far_send, far_recv, swap_send, swap_recv,
     w_sem, load_sem, x_send, x_recv, ring_send, ring_recv,
 ):
@@ -69,7 +71,7 @@
     dev_up, dev_down = device(x, up, z, c), device(x, down, z, c)
     next_z, last_z = device(x, y, lax.rem(z + 1, Z), c), device(x, y, lax.rem(z + Z - 1, Z), c)
     groups = (y, down, up, opposite)
-    bufs = (kb, vb)
+    bufs = (vb, kb)
 
     barrier = pltpu.get_barrier_semaphore()
 
@@ -85,85 +87,127 @@
     loads = [
         pltpu.make_async_copy(source, target, load_sem.at[i])
         for i, (source, target) in enumerate(
-            ((w_hbm, w_rows), (tok_hbm, tok_ref), (bias_hbm, bias_ref), (gate_hbm, gate_ref))
+            (
+                (k_hbm, k_ref), (gk_hbm, gk_ref), (q_hbm, q_ref), (gq_hbm, gq_ref),
+                (stamp_hbm, stamp_ref), (level_hbm, level_ref), (w_hbm, w_rows), (tok_hbm, tok_ref), (bias_hbm, bias_ref), (gate_hbm, gate_ref),
+            )
         )
     ]
     for load in loads:
         load.start()
-    normalize_into(k_ref, gk_ref, kn)
     pl.semaphore_wait(barrier, X * Z - 1 + 3)
 
-    slot = pl.ds(pl.multiple_of((x * Z + z) * ROWS, ROWS), ROWS)
-
-    def scatter(kind, source, target):
-        def send(i, carry):
-            tx, tz = plane_peer(i + 1, x, z)
+    def scatter(kind, p, first, source, target):
+        def send(d, carry):
+            dx, dz = first(d)
+            tx, tz = lax.rem(x + dx, X), lax.rem(z + dz, Z)
             remote(
-                source(tz * X + tx), target, a2a_send.at[kind], a2a_recv.at[kind], device(tx, y, tz, c)
+                source(tz * X + tx), target(dx), a2a_send.at[kind, p], a2a_recv.at[kind, p],
+                device(tx, y, tz, c),
             ).start()
             return carry
 
-        lax.fori_loop(0, X * Z - 1, send, 0)
-        own = pltpu.make_async_copy(source(z * X + x), target, own_sem.at[kind])
+        return send
+
+    def zigzag(k):
+        return jnp.where(lax.rem(k, 2) == 1, (k + 1) // 2, lax.rem(Z - k // 2, Z))
+
+    def scatter_rows(t, source):
+        def target(dx):
+            rows = pl.ds(pl.multiple_of((lax.rem(dx, WIDE) * Z + z) * ROWS, ROWS), ROWS)
+            return bufs[t].at[c, y, dx // WIDE, rows]
+
+        for p in range(PARTS):
+            send = scatter(t, p, lambda d: (p * WIDE + lax.rem(d, WIDE), zigzag(d // WIDE)), source, target)
+            lax.fori_loop(1 if p == 0 else 0, WIDE * Z, send, 0)
+        own = pltpu.make_async_copy(source(z * X + x), target(0), own_sem.at[t])
         own.start()
         return own
 
-    def all_of(kind, sem):
-        rest = kb.at[0, 0, pl.ds(0, GROUP - ROWS)]
-        pltpu.make_async_copy(rest, rest, sem.at[kind]).wait()
-
-    own = [
-        scatter(0, lambda h: kn.at[h], kb.at[c, y, slot]),
-        scatter(1, lambda h: v_ref.at[:, pl.ds(pl.multiple_of(h * HD, HD), HD)], vb.at[c, y, slot]),
-    ]
+    def scatter_query():
+        for hh in range(HALVES):
+            send = scatter(
+                2, hh, lambda d: (lax.rem(d, X), zigzag(d // X)), lambda h: qn.at[h, hh], lambda dx: qb.at[x, hh, z]
+            )
+            lax.fori_loop(1, X * Z, send, 0)
+        own = pltpu.make_async_copy(qn.at[z * X + x], qb.at[x, :, z], own_sem.at[2])
+        own.start()
+        return own
+
+    def all_of(kind, p, sem):
+        rows = QROWS - HROWS if kind == 2 else PART - (ROWS if p == 0 else 0)
+        rest = kb.at[0, 0, 0, pl.ds(0, rows)]
+        pltpu.make_async_copy(rest, rest, sem.at[kind, p]).wait()
+
+    def near(t, i, p):
+        block = bufs[t].at[c, y, p]
+        return remote(block, block, near_send.at[t, i, p], near_recv.at[t, i, p], (dev_up, dev_down)[i])
+
+    def far(t, i):
+        block = bufs[t].at[c, (down, up)[i], i]
+        return remote(block, block, far_send.at[t, i], far_recv.at[t, i], (dev_up, dev_down)[i])
+
+    def swap(t, i, p):
+        block = bufs[t].at[c, groups[i], p]
+        return remote(block, block, swap_send.at[t, i, p], swap_recv.at[t, i, p], partner)
+
+    def pass_own(t, p):
+        if p == 0:
+            own[t].wait()
+        all_of(t, p, a2a_recv)
+        near(t, 0, p).start()
+        near(t, 1, p).start()
+        swap(t, 0, p).start()
+
+    def pass_near(t, p):
+        for i in range(2):
+            near(t, i, p).wait_recv()
+            if i == p:
+                far(t, i).start()
+            swap(t, 1 + i, p).start()
+
+    def pass_far(t):
+        for i in range(2):
+            far(t, i).wait_recv()
+            swap(t, 3, i).start()
+
+    own = [scatter_rows(0, lambda h: v_hbm.at[:, pl.ds(pl.multiple_of(h * HD, HD), HD)])]
+    loads[0].wait()
+    loads[1].wait()
+    normalize_into(k_ref, gk_ref, kn)
+    own.append(scatter_rows(1, lambda h: kn.at[h]))
+    loads[2].wait()
+    loads[3].wait()
     normalize_into(q_ref, gq_ref, qn)
-    own.append(scatter(2, lambda h: qn.at[h], qb.at[x, :, z]))
+    own.append(scatter_query())
+    pass_own(0, 0)
+    pass_own(0, 1)
     w_swap = remote(w_hbm, w_rows, w_sem.at[0], w_sem.at[1], partner)
     w_swap.start()
-
-    half = GROUP // 2
-
-    def near(t, i):
-        block = bufs[t].at[c, y]
-        return remote(block, block, near_send.at[t, i], near_recv.at[t, i], (dev_up, dev_down)[i])
-
-    def far(t, i):
-        block = bufs[t].at[c, (down, up)[i], pl.ds(i * half, half)]
-        return remote(block, block, far_send.at[t, i], far_recv.at[t, i], (dev_up, dev_down)[i])
-
-    def swap(t, i):
-        block = bufs[t].at[c, groups[i]]
-        return remote(block, block, swap_send.at[t, i], swap_recv.at[t, i], partner)
-
-    def pass_own(t):
-        own[t].wait()
-        all_of(t, a2a_recv)
-        near(t, 0).start()
-        near(t, 1).start()
-        swap(t, 0).start()
-
-    def pass_near(t):
-        near(t, 0).wait_recv()
-        far(t, 0).start()
-        swap(t, 1).start()
-        near(t, 1).wait_recv()
-        far(t, 1).start()
-        swap(t, 2).start()
-
-    def pass_far(t):
-        far(t, 0).wait_recv()
-        far(t, 1).wait_recv()
-        swap(t, 3).start()
+    for load in loads[4:6] + loads[7:]:
+        load.wait()
+    level = level_ref[lax.axis_index("frame")]
+    hot = (lax.broadcasted_iota(jnp.int32, (8, gate_ref.shape[0]), 1) == level).astype(jnp.bfloat16)
+    for sub in range(SUBS):
+        where = pl.ds(sub * SUB, SUB)
+        gate_row[:, where] = jnp.dot(hot, gate_ref[:, where], preferred_element_type=jnp.float32)[0:1]
+        bias_row[:, where] = bias_ref[where].astype(jnp.float32)[None]
+    pass_own(1, 0)
+    pass_near(0, 0)
+    pass_own(1, 1)
+    pass_near(0, 1)
 
     def attend(hh, yy):
         query = qb[:, hh].reshape(QROWS, HD)
+        keys = [kb[core, yy].reshape(GROUP, HD) for core in range(2)]
+        values = [vb[core, yy].reshape(GROUP, HD) for core in range(2)]
         scores = [
             lax.dot_general(
-                query, kb[core, yy], (((1,), (1,)), ((), ())), preferred_element_type=jnp.float32
+                query, keys[core], (((1,), (1,)), ((), ())), preferred_element_type=jnp.float32
             )
             for core in range(2)
         ]
-        key_stamp = [stamp_ref[yy * X + f] for f in range(X)]
+        key_stamp = [stamp_ref[yy * X + lax.rem(x + X - f, X)] for f in range(X)]
         summed = [None, None]
         weights = [[], []]
         alphas = []
@@ -175,8 +219,8 @@
             for f in range(X):
                 seen = None
                 for core in range(2):
-                    for i in range(f * KROWS, (f + 1) * KROWS, 128):
-                        tile = scores[core][rows, i : i + 128]
+                    for i in (2 * f, 2 * f + 1):
+                        tile = scores[core][rows, i * 128 : (i + 1) * 128]
                         seen = tile if seen is None else jnp.maximum(seen, tile)
                 best = jnp.maximum(best, seen + shift[f])
             old = top_ref[hh, rows, :]
@@ -187,18 +231,17 @@
             column = new[:, 0:1]
             for core in range(2):
                 row_weights = []
-                for f in range(X):
-                    piece = scores[core][rows, f * KROWS : (f + 1) * KROWS]
-                    exponent = jnp.exp2(piece * SCALE + (shift[f] - column))
-                    for i in range(0, KROWS, 128):
-                        total = total + exponent[:, i : i + 128]
+                for i in range(GROUP // 128):
+                    piece = scores[core][rows, i * 128 : (i + 1) * 128]
+                    exponent = jnp.exp2(piece * SCALE + (shift[i // 2] - column))
+                    total = total + exponent
                     row_weights.append(exponent.astype(jnp.bfloat16))
                 weights[core].append(jnp.concatenate(row_weights, axis=1))
             sum_ref[hh, rows, :] = total
             alphas.append(alpha)
         gained = sum(
             jnp.dot(
-                jnp.concatenate(weights[core], axis=0), vb[core, yy], preferred_element_type=jnp.float32
+                jnp.concatenate(weights[core], axis=0), values[core], preferred_element_type=jnp.float32
             )
             for core in range(2)
         )
@@ -275,27 +318,23 @@
             for way in range(2):
                 ring(hh, way, sub, STEPS - 1).wait_recv()
                 projected = projected + held[hh, way, STEPS - 1, :, where].astype(jnp.float32)
-            gate = jnp.dot(hot, gate_ref[:, where], preferred_element_type=jnp.float32)[0:1]
-            mixed = tok_ref[rows, where].astype(jnp.float32) + gate * (
-                projected + bias_ref[:, where].astype(jnp.float32)
+            mixed = tok_ref[rows, where].astype(jnp.float32) + gate_row[:, where] * (
+                projected + bias_row[:, where]
             )
             out_ref[rows, where] = mixed.astype(jnp.bfloat16)
 
     top_ref[...] = jnp.full_like(top_ref, 2 * HIDDEN)
     sum_ref[...] = jnp.zeros_like(sum_ref)
     acc_ref[...] = jnp.zeros_like(acc_ref)
-    pass_own(0)
-    pass_own(1)
-    pass_near(0)
     own[2].wait()
-    all_of(2, a2a_recv)
-    pass_far(0)
+    all_of(2, 0, a2a_recv)
 
     def wait_swap(i):
-        swap(0, i).wait_recv()
-        swap(1, i).wait_recv()
-
-    order = ((0, 0), (0, 1), (0, 2), (1, 0), (0, 3), (1, 1), (1, 2), (1, 3))
+        for t in range(2):
+            for p in range(PARTS):
+                swap(t, i, p).wait_recv()
+
+    order = ((0, 0), (1, 0), (0, 1), (0, 2), (0, 3), (1, 1), (1, 2), (1, 3))
 
     def choose(i, options):
         value = options[0]
@@ -310,16 +349,22 @@
 
         @pl.when(i == 1)
         def _():
-            pass_near(1)
+            pass_near(1, 0)
+            all_of(2, 1, a2a_recv)
+
+        @pl.when(i == 2)
+        def _():
+            pass_near(1, 1)
+            pass_far(0)
             wait_swap(1)
 
-        @pl.when(i == 2)
+        @pl.when(i == 3)
         def _():
             wait_swap(2)
+            pass_far(1)
 
         @pl.when(i == 4)
         def _():
-            pass_far(1)
             wait_swap(3)
 
         attend(choose(i, [hh for hh, _ in order]), choose(i, [groups[p] for _, p in order]))
@@ -330,8 +375,7 @@
 
         @pl.when(i == 5)
         def _():
-            for load in loads:
-                load.wait()
+            loads[6].wait()
             w_swap.wait()
             project(0)
 
@@ -345,8 +389,6 @@
     finish(1)
     relay(0, 2)
     project(1)
-    level = level_ref[lax.axis_index("frame")]
-    hot = (lax.broadcasted_iota(jnp.int32, (8, gate_ref.shape[0]), 1) == level).astype(jnp.bfloat16)
     relay(0, 3)
     relay(1, 1)
     settle(0)
@@ -356,12 +398,15 @@
 
     for t in range(2):
         for i in range(2):
-            near(t, i).wait_send()
+            for p in range(PARTS):
+                near(t, i, p).wait_send()
             far(t, i).wait_send()
         for i in range(4):
-            swap(t, i).wait_send()
+            for p in range(PARTS):
+                swap(t, i, p).wait_send()
     for kind in range(3):
-        all_of(kind, a2a_send)
+        for p in range(PARTS):
+            all_of(kind, p, a2a_send)
     for hh in range(HALVES):
         for d in range(1, X):
             cross(hh, d).wait_send()
@@ -376,21 +421,26 @@
     out_weight, out_bias, gate_table, noise_level, slot_order,
 ):
     vmem = pl.BlockSpec(memory_space=pltpu.VMEM)
-    hbm = pl.BlockSpec(memory_space=pl.ANY)
-    smem = pl.BlockSpec(memory_space=pltpu.SMEM)
+    hbm = pl.BlockSpec(memory_space=pltpu.HBM)
     bf16, f32 = jnp.bfloat16, jnp.float32
     dma = pltpu.SemaphoreType.DMA
     out = pl.pallas_call(
         fused_kernel,
         out_shape=jax.ShapeDtypeStruct((ROWS, D), bf16),
-        in_specs=[smem, smem] + [vmem] * 5 + [hbm] * 4,
+        in_specs=[hbm] * 11,
         out_specs=vmem,
         scratch_shapes=[
+            pltpu.SMEM((X * Y,), jnp.int32),
+            pltpu.SMEM((X * Y,), jnp.int32),
+            pltpu.VMEM((ROWS, X * Z * HD), bf16),
+            pltpu.VMEM((ROWS, X * Z * HD), bf16),
+            pltpu.VMEM((1, X * Z * HD), f32),
+            pltpu.VMEM((1, X * Z * HD), f32),
             pltpu.VMEM((X * Z, HALVES, HROWS, HD), bf16),
             pltpu.VMEM((X * Z, ROWS, HD), bf16),
             pltpu.VMEM((X, HALVES, Z, HROWS, HD), bf16),
-            pltpu.VMEM((2, Y, GROUP, HD), bf16),
-            pltpu.VMEM((2, Y, GROUP, HD), bf16),
+            pltpu.VMEM((2, Y, PARTS, PART, HD), bf16),
+            pltpu.VMEM((2, Y, PARTS, PART, HD), bf16),
             pltpu.VMEM((HALVES, QROWS, 128), f32),
             pltpu.VMEM((HALVES, QROWS, 128), f32),
             pltpu.VMEM((HALVES, QROWS, HD), f32),
@@ -400,21 +450,28 @@
             pltpu.VMEM((HALVES, FROWS, D), bf16),
             pltpu.VMEM((HALVES, 2, STEPS, HROWS, D), bf16),
             pltpu.VMEM((ROWS, D), bf16),
-            pltpu.VMEM((1, D), bf16),
+            pltpu.VMEM((D,), bf16),
             pltpu.VMEM(gate_table.shape, bf16),
-            dma((3,)), dma((3,)), dma((3,)),
-            dma((2, 2)), dma((2, 2)), dma((2, 2)), dma((2, 2)), dma((2, 4)), dma((2, 4)),
-            dma((2,)), dma((4,)), dma((HALVES, X)), dma((HALVES, X)),
+            pltpu.VMEM((1, D), f32),
+            pltpu.VMEM((1, D), f32),
+            dma((3, PARTS)), dma((3, PARTS)), dma((3,)),
+            dma((2, 2, PARTS)), dma((2, 2, PARTS)), dma((2, 2)), dma((2, 2)), dma((2, 4, PARTS)), dma((2, 4, PARTS)),
+            dma((2,)), dma((10,)), dma((HALVES, X)), dma((HALVES, X)),
             dma((HALVES, 2, SUBS, STEPS)), dma((HALVES, 2, SUBS, STEPS)),
         ],
         compiler_params=pltpu.CompilerParams(
-            collective_id=0, has_side_effects=True, vmem_limit_bytes=56 * 2**20
+            collective_id=0, has_side_effects=True, vmem_limit_bytes=48 * 2**20
         ),
         name="fused",
     )(
-        slot_order.astype(jnp.int32), noise_level.astype(jnp.int32),
-        query_rows[0], key_rows[0], value_rows[0], gain_query[None], gain_key[None],
-        out_weight, tokens[0], out_bias[None], gate_table,
+        *(
+            pltpu.with_memory_space_constraint(array, pltpu.HBM)
+            for array in (
+                slot_order.astype(jnp.int32), noise_level.astype(jnp.int32),
+                query_rows[0], key_rows[0], value_rows[0], gain_query[None], gain_key[None],
+                out_weight, tokens[0], out_bias, gate_table,
+            )
+        )
     )
     return out[None]
 

time: 90 us -> 80.3 us (0.89)
  Pallas kernels: 86 us -> 79.5 us
  local copies, waits for them, and re-layouts: 3.04 us -> 0.73 us
    pallas_call x1, Pallas kernels: 86 us -> 79.5 us  [shards(): pl.pallas_call(fused_kernel, out_shape=jax.ShapeDtypeStruct((ROWS, D), bf...]
    broadcast_in_dim x1 -> x0, local copies, waits for them, and re-layouts: 1.32 us -> none  [shards(): out_bias[None]]
    unnamed x1, local copies, waits for them, and re-layouts: 1.72 us -> 0.73 us
where the time goes in v1:
time: 80.3 us
  Pallas kernels  79.5 us (99%)
    pallas_call x1, Pallas kernels, shards(): pl.pallas_call(fused_kernel, out_shape=jax.ShapeDtypeStruct((ROWS, D), bf...  79.5 us

profile of v1, /device:TPU:24, one launch (start us, length us, event | category | flops | bytes accessed | tf_op | source)
XLA Modules:
  0.0 80.3 jit_solution(3399128031191819796)
XLA Ops:
  0.0 79.5 %fused.1 = bf16[32,5120]{1,0:T(8,128)(2,1)S(1)} custom-call(s32[16]{0:T(128)} %stamp_hbm.1, s32[16]{0:T(128)} %level_hbm.1, bf16[32,4096]{1,0:T(8,128)(2,1)} %bitcast.9, bf16[32,4096]{1,0:T(8,128)(2,1)} %bitcast.10, bf16[32,4096]{1,0:T(8,128)(2,1)} %bitcast.11, f32[1,4096]{1,0:T(1,128)} %bitcast.12, f32[1,4096]{1,0:T(1,128)} %bitcast.13, ...), custom_call_target="tpu_custom_call" | custom-call | tf_op jit(solution)/shard_map/fused/pallas_call | solution.py:427
  79.5 0.7 copy.13

commit v2 on v1

--- a/solution.py
+++ b/solution.py
@@ -16,12 +16,11 @@
 QROWS = X * Z * HROWS
 FROWS = Z * HROWS
 GROUP = X * Z * ROWS
-PARTS = 2
+PARTS = X
 PART = GROUP // PARTS
-WIDE = X // PARTS
 D = 5120
 DEPTH = 512
-SUBS = 4
+SUBS = 2
 SUB = D // SUBS
 STEPS = Z // 2
 MESH = pl.DeviceIdType.MESH
@@ -62,8 +61,8 @@
     stamp_hbm, level_hbm, q_hbm, k_hbm, v_hbm, gq_hbm, gk_hbm, w_hbm, tok_hbm, bias_hbm, gate_hbm,
     out_ref,
     stamp_ref, level_ref, q_ref, k_ref, gq_ref, gk_ref, qn, kn, qb, kb, vb, top_ref, sum_ref, acc_ref, att, a_ref, w_ref, part, held, tok_ref, bias_ref, gate_ref, bias_row, gate_row,
-    a2a_send, a2a_recv, own_sem, near_send, near_recv, far_send, far_recv, swap_send, swap_recv,
-    w_sem, load_sem, x_send, x_recv, ring_send, ring_recv,
+    a2a_send, a2a_recv, own_sem, ring_y_send, near_recv, far_recv, swap_send, swap_recv,
+    w_sem, load_sem, x_send, x_own, x_recv, ring_send, ring_recv,
 ):
     x, y, z, c = position()
     up, down, opposite = lax.rem(y + 1, Y), lax.rem(y + Y - 1, Y), lax.rem(y + 2, Y)
@@ -102,24 +101,23 @@
             dx, dz = first(d)
             tx, tz = lax.rem(x + dx, X), lax.rem(z + dz, Z)
             remote(
-                source(tz * X + tx), target(dx), a2a_send.at[kind, p], a2a_recv.at[kind, p],
+                source(tz * X + tx), target(dx), a2a_send.at[kind], a2a_recv.at[kind, p],
                 device(tx, y, tz, c),
             ).start()
             return carry
 
         return send
 
-    def zigzag(k):
-        return jnp.where(lax.rem(k, 2) == 1, (k + 1) // 2, lax.rem(Z - k // 2, Z))
+    def farthest_first(k):
+        return jnp.where(lax.rem(k, 2) == 1, (Z - 1 - k) // 2, lax.rem(Z // 2 + k // 2, Z))
 
     def scatter_rows(t, source):
         def target(dx):
-            rows = pl.ds(pl.multiple_of((lax.rem(dx, WIDE) * Z + z) * ROWS, ROWS), ROWS)
-            return bufs[t].at[c, y, dx // WIDE, rows]
+            return bufs[t].at[c, y, dx, pl.ds(pl.multiple_of(z * ROWS, ROWS), ROWS)]
 
         for p in range(PARTS):
-            send = scatter(t, p, lambda d: (p * WIDE + lax.rem(d, WIDE), zigzag(d // WIDE)), source, target)
-            lax.fori_loop(1 if p == 0 else 0, WIDE * Z, send, 0)
+            send = scatter(t, p, lambda k: (p, farthest_first(k)), source, target)
+            lax.fori_loop(0, Z - 1 if p == 0 else Z, send, 0)
         own = pltpu.make_async_copy(source(z * X + x), target(0), own_sem.at[t])
         own.start()
         return own
@@ -127,34 +125,38 @@
     def scatter_query():
         for hh in range(HALVES):
             send = scatter(
-                2, hh, lambda d: (lax.rem(d, X), zigzag(d // X)), lambda h: qn.at[h, hh], lambda dx: qb.at[x, hh, z]
-            )
-            lax.fori_loop(1, X * Z, send, 0)
+                2, hh, lambda d: (lax.rem(d + 1, X), farthest_first(d // X)),
+                lambda h: qn.at[h, hh], lambda dx: qb.at[x, hh, z],
+            )
+            lax.fori_loop(0, X * Z - 1, send, 0)
         own = pltpu.make_async_copy(qn.at[z * X + x], qb.at[x, :, z], own_sem.at[2])
         own.start()
         return own
 
-    def all_of(kind, p, sem):
-        rows = QROWS - HROWS if kind == 2 else PART - (ROWS if p == 0 else 0)
-        rest = kb.at[0, 0, 0, pl.ds(0, rows)]
-        pltpu.make_async_copy(rest, rest, sem.at[kind, p]).wait()
+    def arrived(kind, p):
+        if kind == 2:
+            rest = qn.at[pl.ds(0, X * Z - 1), 0]
+        else:
+            rest = kb.at[0, 0, 0, pl.ds(0, PART - (ROWS if p == 0 else 0))]
+        pltpu.make_async_copy(rest, rest, a2a_recv.at[kind, p]).wait()
 
     def near(t, i, p):
         block = bufs[t].at[c, y, p]
-        return remote(block, block, near_send.at[t, i, p], near_recv.at[t, i, p], (dev_up, dev_down)[i])
-
-    def far(t, i):
-        block = bufs[t].at[c, (down, up)[i], i]
-        return remote(block, block, far_send.at[t, i], far_recv.at[t, i], (dev_up, dev_down)[i])
+        return remote(block, block, ring_y_send, near_recv.at[t, i, p], (dev_up, dev_down)[i])
+
+    def far(t, p):
+        i = 2 * p // PARTS
+        block = bufs[t].at[c, (down, up)[i], p]
+        return remote(block, block, ring_y_send, far_recv.at[t, p], (dev_up, dev_down)[i])
 
     def swap(t, i, p):
         block = bufs[t].at[c, groups[i], p]
-        return remote(block, block, swap_send.at[t, i, p], swap_recv.at[t, i, p], partner)
+        return remote(block, block, swap_send, swap_recv.at[i], partner)
 
     def pass_own(t, p):
         if p == 0:
             own[t].wait()
-        all_of(t, p, a2a_recv)
+        arrived(t, p)
         near(t, 0, p).start()
         near(t, 1, p).start()
         swap(t, 0, p).start()
@@ -162,16 +164,22 @@
     def pass_near(t, p):
         for i in range(2):
             near(t, i, p).wait_recv()
-            if i == p:
-                far(t, i).start()
+            if i == 2 * p // PARTS:
+                far(t, p).start()
             swap(t, 1 + i, p).start()
 
     def pass_far(t):
-        for i in range(2):
-            far(t, i).wait_recv()
-            swap(t, 3, i).start()
+        for p in (0, PARTS // 2, 1, PARTS // 2 + 1):
+            far(t, p).wait_recv()
+            swap(t, 3, p).start()
+
+    def wait_swap(i):
+        both = kb.at[:, 0]
+        pltpu.make_async_copy(both, both, swap_recv.at[i]).wait()
 
     own = [scatter_rows(0, lambda h: v_hbm.at[:, pl.ds(pl.multiple_of(h * HD, HD), HD)])]
+    w_swap = remote(w_hbm, w_rows, w_sem.at[0], w_sem.at[1], partner)
+    w_swap.start()
     loads[0].wait()
     loads[1].wait()
     normalize_into(k_ref, gk_ref, kn)
@@ -180,10 +188,8 @@
     loads[3].wait()
     normalize_into(q_ref, gq_ref, qn)
     own.append(scatter_query())
-    pass_own(0, 0)
-    pass_own(0, 1)
-    w_swap = remote(w_hbm, w_rows, w_sem.at[0], w_sem.at[1], partner)
-    w_swap.start()
+    for p in range(PARTS):
+        pass_own(0, p)
     for load in loads[4:6] + loads[7:]:
         load.wait()
     level = level_ref[lax.axis_index("frame")]
@@ -192,10 +198,10 @@
         where = pl.ds(sub * SUB, SUB)
         gate_row[:, where] = jnp.dot(hot, gate_ref[:, where], preferred_element_type=jnp.float32)[0:1]
         bias_row[:, where] = bias_ref[where].astype(jnp.float32)[None]
-    pass_own(1, 0)
-    pass_near(0, 0)
-    pass_own(1, 1)
-    pass_near(0, 1)
+    for p in range(PARTS):
+        pass_own(1, p)
+    for p in range(PARTS):
+        pass_near(0, p)
 
     def attend(hh, yy):
         query = qb[:, hh].reshape(QROWS, HD)
@@ -251,12 +257,12 @@
         tx = lax.rem(x + d, X)
         columns = pl.ds(pl.multiple_of(x * HD, HD), HD)
         return remote(
-            att.at[hh, tx], a_ref.at[hh, :, columns], x_send.at[hh, d], x_recv.at[hh, d], device(tx, y, z, c)
+            att.at[hh, tx], a_ref.at[hh, :, columns], x_send, x_recv.at[hh], device(tx, y, z, c)
         )
 
     def cross_own(hh):
         columns = pl.ds(pl.multiple_of(x * HD, HD), HD)
-        return pltpu.make_async_copy(att.at[hh, x], a_ref.at[hh, :, columns], x_send.at[hh, 0])
+        return pltpu.make_async_copy(att.at[hh, x], a_ref.at[hh, :, columns], x_own.at[hh])
 
     def finish(hh):
         total = jnp.sum(sum_ref[hh], axis=-1, keepdims=True)
@@ -280,15 +286,15 @@
             source = held.at[hh, way, step - 1, :, where]
         at = (hh, way, sub, step)
         return remote(
-            source, held.at[hh, way, step, :, where], ring_send.at[at], ring_recv.at[at], (next_z, last_z)[way]
+            source, held.at[hh, way, step, :, where], ring_send.at[hh], ring_recv.at[at], (next_z, last_z)[way]
         )
 
     pairs = [(way, sub) for sub in range(SUBS // 2) for way, sub in ((0, sub), (1, sub + SUBS // 2))]
     pairs += [(1 - way, sub) for way, sub in pairs]
 
     def project(hh):
-        for d in range(1, X):
-            cross(hh, d).wait_recv()
+        three = att.at[hh, pl.ds(0, X - 1)]
+        pltpu.make_async_copy(three, three, x_recv.at[hh]).wait()
         cross_own(hh).wait()
         for sub in range(SUBS):
             where = pl.ds(sub * SUB, SUB)
@@ -326,13 +332,10 @@
     top_ref[...] = jnp.full_like(top_ref, 2 * HIDDEN)
     sum_ref[...] = jnp.zeros_like(sum_ref)
     acc_ref[...] = jnp.zeros_like(acc_ref)
+    pass_near(1, 0)
     own[2].wait()
-    all_of(2, 0, a2a_recv)
-
-    def wait_swap(i):
-        for t in range(2):
-            for p in range(PARTS):
-                swap(t, i, p).wait_recv()
+    arrived(2, 0)
+    pass_near(1, 1)
 
     order = ((0, 0), (1, 0), (0, 1), (0, 2), (0, 3), (1, 1), (1, 2), (1, 3))
 
@@ -349,12 +352,12 @@
 
         @pl.when(i == 1)
         def _():
-            pass_near(1, 0)
-            all_of(2, 1, a2a_recv)
+            pass_near(1, 2)
+            pass_near(1, 3)
+            arrived(2, 1)
 
         @pl.when(i == 2)
         def _():
-            pass_near(1, 1)
             pass_far(0)
             wait_swap(1)
 
@@ -396,24 +399,16 @@
     relay(1, 3)
     settle(1)
 
-    for t in range(2):
-        for i in range(2):
-            for p in range(PARTS):
-                near(t, i, p).wait_send()
-            far(t, i).wait_send()
-        for i in range(4):
-            for p in range(PARTS):
-                swap(t, i, p).wait_send()
+    def drain(ref, sem):
+        pltpu.make_async_copy(ref, ref, sem).wait()
+
     for kind in range(3):
-        for p in range(PARTS):
-            all_of(kind, p, a2a_send)
+        drain(kn.at[pl.ds(0, X * Z - 1)], a2a_send.at[kind])
+    drain(kb.at[:, pl.ds(0, 3)], ring_y_send)
+    drain(kb, swap_send)
+    drain(att.at[:, pl.ds(0, X - 1)], x_send)
     for hh in range(HALVES):
-        for d in range(1, X):
-            cross(hh, d).wait_send()
-        for way in range(2):
-            for sub in range(SUBS):
-                for s in range(opens(way, sub), STEPS):
-                    ring(hh, way, sub, s).wait_send()
+        drain(held.at[hh, :, :, :, pl.ds(0, D - D // (2 * STEPS))], ring_send.at[hh])
 
 
 def shards(
@@ -454,10 +449,9 @@
             pltpu.VMEM(gate_table.shape, bf16),
             pltpu.VMEM((1, D), f32),
             pltpu.VMEM((1, D), f32),
-            dma((3, PARTS)), dma((3, PARTS)), dma((3,)),
-            dma((2, 2, PARTS)), dma((2, 2, PARTS)), dma((2, 2)), dma((2, 2)), dma((2, 4, PARTS)), dma((2, 4, PARTS)),
-            dma((2,)), dma((10,)), dma((HALVES, X)), dma((HALVES, X)),
-            dma((HALVES, 2, SUBS, STEPS)), dma((HALVES, 2, SUBS, STEPS)),
+            dma((3,)), dma((3, PARTS)), dma((3,)), dma(()), dma((2, 2, PARTS)), dma((2, PARTS)), dma(()), dma((4,)),
+            dma((2,)), dma((10,)), dma(()), dma((HALVES,)), dma((HALVES,)),
+            dma((HALVES,)), dma((HALVES, 2, SUBS, STEPS)),
         ],
         compiler_params=pltpu.CompilerParams(
             collective_id=0, has_side_effects=True, vmem_limit_bytes=48 * 2**20

time: 80.3 us -> 76.8 us (0.956)
  Pallas kernels: 79.5 us -> 75.6 us
    pallas_call x1, Pallas kernels: 79.5 us -> 75.6 us  [shards(): pl.pallas_call(fused_kernel, out_shape=jax.ShapeDtypeStruct((ROWS, D), bf...]
where the time goes in v2:
time: 76.8 us; the launch traced here: 76.4 us
  Pallas kernels  75.6 us (98%)
    pallas_call x1, Pallas kernels, shards(): pl.pallas_call(fused_kernel, out_shape=jax.ShapeDtypeStruct((ROWS, D), bf...  75.6 us

profile of v2, /device:TPU:24, one launch (start us, length us, event | category | flops | bytes accessed | tf_op | source)
XLA Modules:
  0.0 76.4 jit_solution(18390479912820290477)
XLA Ops:
  0.0 75.6 %fused.1 = bf16[32,5120]{1,0:T(8,128)(2,1)S(1)} custom-call(s32[16]{0:T(128)} %stamp_hbm.1, s32[16]{0:T(128)} %level_hbm.1, bf16[32,4096]{1,0:T(8,128)(2,1)} %bitcast.9, bf16[32,4096]{1,0:T(8,128)(2,1)} %bitcast.10, bf16[32,4096]{1,0:T(8,128)(2,1)} %bitcast.11, f32[1,4096]{1,0:T(1,128)} %bitcast.12, f32[1,4096]{1,0:T(1,128)} %bitcast.13, ...), custom_call_target="tpu_custom_call" | custom-call | tf_op jit(solution)/shard_map/fused/pallas_call | solution.py:422
  75.6 0.7 copy.13

commit v3 on v2

--- a/solution.py
+++ b/solution.py
@@ -20,7 +20,7 @@
 PART = GROUP // PARTS
 D = 5120
 DEPTH = 512
-SUBS = 2
+SUBS = 4
 SUB = D // SUBS
 STEPS = Z // 2
 MESH = pl.DeviceIdType.MESH
@@ -42,10 +42,6 @@
     return pltpu.make_async_remote_copy(
         src_ref=src, dst_ref=dst, send_sem=send, recv_sem=recv, device_id=dev, device_id_type=MESH
     )
-
-
-def plane_peer(d, x, z):
-    return lax.rem(x + lax.rem(d, X), X), lax.rem(z + d // X, Z)
 
 
 def normalize_into(rows_ref, gain_ref, out_ref):
@@ -72,10 +68,13 @@
     groups = (y, down, up, opposite)
     bufs = (vb, kb)
 
+    def farthest_first(k):
+        return jnp.where(lax.rem(k, 2) == 1, (Z - 1 - k) // 2, lax.rem(Z // 2 + k // 2, Z))
+
     barrier = pltpu.get_barrier_semaphore()
 
     def greet(i, carry):
-        tx, tz = plane_peer(i + 1, x, z)
+        tx, tz = lax.rem(x + i + 1, X), lax.rem(z + farthest_first(i // X), Z)
         pl.semaphore_signal(barrier, inc=1, device_id=device(tx, y, tz, c), device_id_type=MESH)
         return carry
 
@@ -107,9 +106,6 @@
             return carry
 
         return send
-
-    def farthest_first(k):
-        return jnp.where(lax.rem(k, 2) == 1, (Z - 1 - k) // 2, lax.rem(Z // 2 + k // 2, Z))
 
     def scatter_rows(t, source):
         def target(dx):
@@ -296,14 +292,14 @@
         three = att.at[hh, pl.ds(0, X - 1)]
         pltpu.make_async_copy(three, three, x_recv.at[hh]).wait()
         cross_own(hh).wait()
-        for sub in range(SUBS):
+        for way, sub in pairs[:SUBS]:
             where = pl.ds(sub * SUB, SUB)
             part[hh, :, where] = jnp.dot(
                 a_ref[hh], w_ref[:, where], preferred_element_type=jnp.float32
             ).astype(jnp.bfloat16)
-            ring(hh, sub // (SUBS // 2), sub, 0).start()
-        for sub in range(SUBS):
-            ring(hh, 1 - sub // (SUBS // 2), sub, 1).start()
+            ring(hh, way, sub, 0).start()
+        for way, sub in pairs[SUBS:]:
+            ring(hh, way, sub, 1).start()
 
     def relay(hh, step):
         for way, sub in pairs:
@@ -376,27 +372,24 @@
         def _():
             finish(0)
 
-        @pl.when(i == 5)
+        @pl.when(i == 6)
         def _():
             loads[6].wait()
             w_swap.wait()
             project(0)
 
-        @pl.when(i == 6)
-        def _():
-            relay(0, 1)
-
         return carry
 
     lax.fori_loop(0, len(order), step, 0)
     finish(1)
+    relay(0, 1)
+    project(1)
+    relay(1, 1)
     relay(0, 2)
-    project(1)
+    relay(1, 2)
     relay(0, 3)
-    relay(1, 1)
+    relay(1, 3)
     settle(0)
-    relay(1, 2)
-    relay(1, 3)
     settle(1)
 
     def drain(ref, sem):

time: 76.8 us -> 74.4 us (0.969)
  Pallas kernels: 75.6 us -> 72.9 us
    pallas_call x1, Pallas kernels: 75.6 us -> 72.9 us  [shards(): pl.pallas_call(fused_kernel, out_shape=jax.ShapeDtypeStruct((ROWS, D), bf...]
where the time goes in v3:
time: 74.4 us; the launch traced here: 73.7 us
  Pallas kernels  72.9 us (98%)
    pallas_call x1, Pallas kernels, shards(): pl.pallas_call(fused_kernel, out_shape=jax.ShapeDtypeStruct((ROWS, D), bf...  72.9 us

profile of v3, /device:TPU:24, one launch (start us, length us, event | category | flops | bytes accessed | tf_op | source)
XLA Modules:
  0.0 73.7 jit_solution(7683518277051370479)
XLA Ops:
  0.0 72.9 %fused.1 = bf16[32,5120]{1,0:T(8,128)(2,1)S(1)} custom-call(s32[16]{0:T(128)} %stamp_hbm.1, s32[16]{0:T(128)} %level_hbm.1, bf16[32,4096]{1,0:T(8,128)(2,1)} %bitcast.9, bf16[32,4096]{1,0:T(8,128)(2,1)} %bitcast.10, bf16[32,4096]{1,0:T(8,128)(2,1)} %bitcast.11, f32[1,4096]{1,0:T(1,128)} %bitcast.12, f32[1,4096]{1,0:T(1,128)} %bitcast.13, ...), custom_call_target="tpu_custom_call" | custom-call | tf_op jit(solution)/shard_map/fused/pallas_call | solution.py:415
  72.9 0.7 copy.13

commit v4 on v3

--- a/solution.py
+++ b/solution.py
@@ -69,16 +69,17 @@
     bufs = (vb, kb)
 
     def farthest_first(k):
+        if isinstance(k, int):
+            return (Z - 1 - k) // 2 if k % 2 else (Z // 2 + k // 2) % Z
         return jnp.where(lax.rem(k, 2) == 1, (Z - 1 - k) // 2, lax.rem(Z // 2 + k // 2, Z))
 
     barrier = pltpu.get_barrier_semaphore()
 
-    def greet(i, carry):
-        tx, tz = lax.rem(x + i + 1, X), lax.rem(z + farthest_first(i // X), Z)
-        pl.semaphore_signal(barrier, inc=1, device_id=device(tx, y, tz, c), device_id_type=MESH)
-        return carry
-
-    lax.fori_loop(0, X * Z - 1, greet, 0)
+    for dz in (4, 3, 5, 2, 6, 1, 7, 0):
+        for dx in (2, 1, 3, 0):
+            if dx or dz:
+                peer = device(lax.rem(x + dx, X), y, lax.rem(z + dz, Z), c)
+                pl.semaphore_signal(barrier, inc=1, device_id=peer, device_id_type=MESH)
     for dev in (dev_up, dev_down, partner):
         pl.semaphore_signal(barrier, inc=1, device_id=dev, device_id_type=MESH)
     w_rows = w_ref.at[pl.ds(pl.multiple_of(c * (DEPTH // 2), DEPTH // 2), DEPTH // 2)]
@@ -113,7 +114,8 @@
 
         for p in range(PARTS):
             send = scatter(t, p, lambda k: (p, farthest_first(k)), source, target)
-            lax.fori_loop(0, Z - 1 if p == 0 else Z, send, 0)
+            for k in range(Z - 1 if p == 0 else Z):
+                send(k, 0)
         own = pltpu.make_async_copy(source(z * X + x), target(0), own_sem.at[t])
         own.start()
         return own
@@ -138,7 +140,7 @@
 
     def near(t, i, p):
         block = bufs[t].at[c, y, p]
-        return remote(block, block, ring_y_send, near_recv.at[t, i, p], (dev_up, dev_down)[i])
+        return remote(block, block, ring_y_send, near_recv.at[t, p], (dev_up, dev_down)[i])
 
     def far(t, p):
         i = 2 * p // PARTS
@@ -158,11 +160,11 @@
         swap(t, 0, p).start()
 
     def pass_near(t, p):
-        for i in range(2):
-            near(t, i, p).wait_recv()
-            if i == 2 * p // PARTS:
-                far(t, p).start()
-            swap(t, 1 + i, p).start()
+        pair = kb.at[0, 0, pl.ds(0, 2)]
+        pltpu.make_async_copy(pair, pair, near_recv.at[t, p]).wait()
+        far(t, p).start()
+        swap(t, 1, p).start()
+        swap(t, 2, p).start()
 
     def pass_far(t):
         for p in (0, PARTS // 2, 1, PARTS // 2 + 1):
@@ -199,53 +201,54 @@
     for p in range(PARTS):
         pass_near(0, p)
 
-    def attend(hh, yy):
+    def attend(hh, groups_seen):
         query = qb[:, hh].reshape(QROWS, HD)
-        keys = [kb[core, yy].reshape(GROUP, HD) for core in range(2)]
-        values = [vb[core, yy].reshape(GROUP, HD) for core in range(2)]
+        pieces = [(yy, core) for yy in groups_seen for core in range(2)]
         scores = [
             lax.dot_general(
-                query, keys[core], (((1,), (1,)), ((), ())), preferred_element_type=jnp.float32
-            )
-            for core in range(2)
+                query, kb[core, yy].reshape(GROUP, HD), (((1,), (1,)), ((), ())),
+                preferred_element_type=jnp.float32,
+            )
+            for yy, core in pieces
         ]
-        key_stamp = [stamp_ref[yy * X + lax.rem(x + X - f, X)] for f in range(X)]
-        summed = [None, None]
-        weights = [[], []]
+        stamps = [[stamp_ref[yy * X + lax.rem(x + X - f, X)] for f in range(X)] for yy in groups_seen]
+        weights = [[] for _ in pieces]
         alphas = []
         for g in range(X):
             stamp = stamp_ref[y * X + g]
             rows = slice(g * FROWS, (g + 1) * FROWS)
             best = jnp.full((FROWS, 128), 2 * HIDDEN, jnp.float32)
-            shift = [jnp.where(key_stamp[f] <= stamp, 0.0, HIDDEN) for f in range(X)]
-            for f in range(X):
-                seen = None
-                for core in range(2):
-                    for i in (2 * f, 2 * f + 1):
-                        tile = scores[core][rows, i * 128 : (i + 1) * 128]
-                        seen = tile if seen is None else jnp.maximum(seen, tile)
-                best = jnp.maximum(best, seen + shift[f])
+            shift = [[jnp.where(key <= stamp, 0.0, HIDDEN) for key in keys] for keys in stamps]
+            for n in range(len(groups_seen)):
+                for f in range(X):
+                    seen = None
+                    for score in scores[2 * n : 2 * n + 2]:
+                        for i in (2 * f, 2 * f + 1):
+                            tile = score[rows, i * 128 : (i + 1) * 128]
+                            seen = tile if seen is None else jnp.maximum(seen, tile)
+                    best = jnp.maximum(best, seen + shift[n][f])
             old = top_ref[hh, rows, :]
             new = jnp.maximum(old, jnp.max(best, axis=-1, keepdims=True) * SCALE)
             alpha = jnp.exp2(old - new)
             top_ref[hh, rows, :] = new
             total = sum_ref[hh, rows, :] * alpha
             column = new[:, 0:1]
-            for core in range(2):
+            for m, score in enumerate(scores):
                 row_weights = []
                 for i in range(GROUP // 128):
-                    piece = scores[core][rows, i * 128 : (i + 1) * 128]
-                    exponent = jnp.exp2(piece * SCALE + (shift[i // 2] - column))
+                    piece = score[rows, i * 128 : (i + 1) * 128]
+                    exponent = jnp.exp2(piece * SCALE + (shift[m // 2][i // 2] - column))
                     total = total + exponent
                     row_weights.append(exponent.astype(jnp.bfloat16))
-                weights[core].append(jnp.concatenate(row_weights, axis=1))
+                weights[m].append(jnp.concatenate(row_weights, axis=1))
             sum_ref[hh, rows, :] = total
             alphas.append(alpha)
         gained = sum(
             jnp.dot(
-                jnp.concatenate(weights[core], axis=0), values[core], preferred_element_type=jnp.float32
-            )
-            for core in range(2)
+                jnp.concatenate(weights[m], axis=0), vb[core, yy].reshape(GROUP, HD),
+                preferred_element_type=jnp.float32,
+            )
+            for m, (yy, core) in enumerate(pieces)
         )
         acc_ref[hh] = acc_ref[hh] * jnp.concatenate(alphas, axis=0) + gained
 
@@ -333,7 +336,7 @@
     arrived(2, 0)
     pass_near(1, 1)
 
-    order = ((0, 0), (1, 0), (0, 1), (0, 2), (0, 3), (1, 1), (1, 2), (1, 3))
+    order = ((0, 0), (1, 0), (0, 1), (0, 2), (0, 3))
 
     def choose(i, options):
         value = options[0]
@@ -366,24 +369,19 @@
         def _():
             wait_swap(3)
 
-        attend(choose(i, [hh for hh, _ in order]), choose(i, [groups[p] for _, p in order]))
-
-        @pl.when(i == 4)
-        def _():
-            finish(0)
-
-        @pl.when(i == 6)
-        def _():
-            loads[6].wait()
-            w_swap.wait()
-            project(0)
+        attend(choose(i, [hh for hh, _ in order]), [choose(i, [groups[p] for _, p in order])])
 
         return carry
 
     lax.fori_loop(0, len(order), step, 0)
+    finish(0)
+    attend(1, (down, up, opposite))
     finish(1)
+    loads[6].wait()
+    w_swap.wait()
+    project(0)
+    project(1)
     relay(0, 1)
-    project(1)
     relay(1, 1)
     relay(0, 2)
     relay(1, 2)
@@ -442,7 +440,7 @@
             pltpu.VMEM(gate_table.shape, bf16),
             pltpu.VMEM((1, D), f32),
             pltpu.VMEM((1, D), f32),
-            dma((3,)), dma((3, PARTS)), dma((3,)), dma(()), dma((2, 2, PARTS)), dma((2, PARTS)), dma(()), dma((4,)),
+            dma((3,)), dma((3, PARTS)), dma((3,)), dma(()), dma((2, PARTS)), dma((2, PARTS)), dma(()), dma((4,)),
             dma((2,)), dma((10,)), dma(()), dma((HALVES,)), dma((HALVES,)),
             dma((HALVES,)), dma((HALVES, 2, SUBS, STEPS)),
         ],

time: 74.4 us -> 73.7 us (level)
  Pallas kernels: 72.9 us -> 72.1 us
    pallas_call x1, Pallas kernels: 72.9 us -> 72.1 us  [shards(): pl.pallas_call(fused_kernel, out_shape=jax.ShapeDtypeStruct((ROWS, D), bf...]
where the time goes in v4:
time: 73.7 us; the launch traced here: 72.8 us
  Pallas kernels  72.1 us (98%)
    pallas_call x1, Pallas kernels, shards(): pl.pallas_call(fused_kernel, out_shape=jax.ShapeDtypeStruct((ROWS, D), bf...  72.1 us

profile of v4, /device:TPU:24, one launch (start us, length us, event | category | flops | bytes accessed | tf_op | source)
XLA Modules:
  0.0 72.8 jit_solution(3889224085414948877)
XLA Ops:
  0.0 72.1 %fused.1 = bf16[32,5120]{1,0:T(8,128)(2,1)S(1)} custom-call(s32[16]{0:T(128)} %stamp_hbm.1, s32[16]{0:T(128)} %level_hbm.1, bf16[32,4096]{1,0:T(8,128)(2,1)} %bitcast.9, bf16[32,4096]{1,0:T(8,128)(2,1)} %bitcast.10, bf16[32,4096]{1,0:T(8,128)(2,1)} %bitcast.11, f32[1,4096]{1,0:T(1,128)} %bitcast.12, f32[1,4096]{1,0:T(1,128)} %bitcast.13, ...), custom_call_target="tpu_custom_call" | custom-call | tf_op jit(solution)/shard_map/fused/pallas_call | solution.py:413
  72.1 0.7 copy.13

commit v5 on v4

--- a/solution.py
+++ b/solution.py
@@ -336,44 +336,26 @@
     arrived(2, 0)
     pass_near(1, 1)
 
-    order = ((0, 0), (1, 0), (0, 1), (0, 2), (0, 3))
-
-    def choose(i, options):
-        value = options[0]
-        for n in range(1, len(options)):
-            value = jnp.where(i == n, options[n], value)
-        return value
-
-    def step(i, carry):
-        @pl.when(i == 0)
-        def _():
-            wait_swap(0)
-
-        @pl.when(i == 1)
+    wait_swap(0)
+
+    def opening(hh, carry):
+        @pl.when(hh == 1)
         def _():
             pass_near(1, 2)
             pass_near(1, 3)
             arrived(2, 1)
 
-        @pl.when(i == 2)
-        def _():
-            pass_far(0)
-            wait_swap(1)
-
-        @pl.when(i == 3)
-        def _():
-            wait_swap(2)
-            pass_far(1)
-
-        @pl.when(i == 4)
-        def _():
-            wait_swap(3)
-
-        attend(choose(i, [hh for hh, _ in order]), [choose(i, [groups[p] for _, p in order])])
-
+        attend(hh, (y,))
         return carry
 
-    lax.fori_loop(0, len(order), step, 0)
+    lax.fori_loop(0, HALVES, opening, 0)
+    pass_far(0)
+    wait_swap(1)
+    wait_swap(2)
+    pass_far(1)
+    attend(0, (down, up))
+    wait_swap(3)
+    attend(0, (opposite,))
     finish(0)
     attend(1, (down, up, opposite))
     finish(1)

time: 73.7 us -> 73.9 us (level)
  no operation moved by 1% of the time
where the time goes in v5:
time: 73.9 us; the launch traced here: 73.1 us
  Pallas kernels  72.4 us (98%)
    pallas_call x1, Pallas kernels, shards(): pl.pallas_call(fused_kernel, out_shape=jax.ShapeDtypeStruct((ROWS, D), bf...  72.4 us

profile of v5, /device:TPU:24, one launch (start us, length us, event | category | flops | bytes accessed | tf_op | source)
XLA Modules:
  0.0 73.1 jit_solution(17477548172878735431)
XLA Ops:
  0.0 72.4 %fused.1 = bf16[32,5120]{1,0:T(8,128)(2,1)S(1)} custom-call(s32[16]{0:T(128)} %stamp_hbm.1, s32[16]{0:T(128)} %level_hbm.1, bf16[32,4096]{1,0:T(8,128)(2,1)} %bitcast.9, bf16[32,4096]{1,0:T(8,128)(2,1)} %bitcast.10, bf16[32,4096]{1,0:T(8,128)(2,1)} %bitcast.11, f32[1,4096]{1,0:T(1,128)} %bitcast.12, f32[1,4096]{1,0:T(1,128)} %bitcast.13, ...), custom_call_target="tpu_custom_call" | custom-call | tf_op jit(solution)/shard_map/fused/pallas_call | solution.py:395
  72.4 0.7 copy.13
